TPU v7x, 256 devices: a whole 4x4x8 slice. The times are simulated.
256 devices in a mesh: dp: 32 (over z_lo, x, core), mp: 8 (over z_hi, y).
Axes of the slice: x: 4, y: 4, z: 8 (z_hi: 2, z_lo: 4; z = z_hi * 4 + z_lo), core: 2. Of those that a mesh axis runs over, the one named last changes fastest.
Arguments:
- clean: bfloat16 [32, 1024, 1280], P('dp', 'mp'), may hold values from -6 to 6
- noise: bfloat16 [32, 1024, 1280], P('dp', 'mp'), may hold values from -6 to 6
- tsteps: int32 [32], P('dp'), may hold values from 0 to 999
- alpha_tab: float32 [1000], replicated, may hold values from 0.3 to 0.99
- weight_tab: float32 [1000], replicated, may hold values from 0.1 to 3
- norm1_gain: float32 [1280], replicated, may hold values from 0.1 to 1.9
- norm2_gain: float32 [1280], replicated, may hold values from 0.1 to 1.9
- wqkv: bfloat16 [3, 1280, 1280], P(None, 'dp', 'mp'), may hold values from -4 to 4
- wout: bfloat16 [1280, 1280], P('dp', 'mp'), may hold values from -0.625 to 0.625
- wgate: bfloat16 [1280, 5120], P('dp', 'mp'), may hold values from -0.15625 to 0.15625
- wvalue: bfloat16 [1280, 5120], P('dp', 'mp'), may hold values from -0.15625 to 0.15625
- wdown: bfloat16 [5120, 1280], P('mp', 'dp'), may hold values from -0.078125 to 0.078125
Outputs:
- denoised: float32 [32, 1024, 1280], P('dp', 'mp')
- loss: float32 [], replicated
All inputs are finite; a program needn't handle non-finite values.
Results may differ from a plain program's by a relative error of at most 0.02.
Values may be sent and summed in bfloat16 or wider, within the bound.
A program may use at most 64 MiB of HBM per device.

v0:
```python
import jax
import jax.numpy as jnp
from jax import lax
from jax.sharding import Mesh
from jax.sharding import PartitionSpec as P

D = 1280
HEADS = 20
HEAD = 64
L = 1024
MP = ("mp_0", "mp_1")
DP = ("dp_0", "dp_1", "dp_2")
DP_MP = ("dp_0", "dp_1", "dp_2", "mp_0", "mp_1")


def copy_for_each(value, axis):
    length = lax.axis_size(axis)
    return lax.all_to_all(
        jnp.broadcast_to(value[None], (length, *value.shape)), axis, 0, 0, tiled=True
    )


def in_order(blocks, dim):
    blocks = jnp.moveaxis(blocks, 0, dim)
    dims = blocks.shape
    return blocks.reshape(*dims[:dim], dims[dim] * dims[dim + 1], *dims[dim + 2 :])


def gathered_copies(value, axis, dim):
    blocks = copy_for_each(value, axis)
    return in_order(blocks, dim)


def sent_together(arrays, axis, dim, along):
    ends, at = ([], 0)
    for a in arrays[:-1]:
        at += a.shape[along]
        ends.append(at)
    both = jnp.concatenate(arrays, axis=along)
    return tuple(jnp.split(lax.all_gather(both, axis, axis=dim, tiled=True), ends, axis=along))


def whole_of(value, axes, dim):
    far, near = axes
    blocks = copy_for_each(copy_for_each(value, far), near)
    return in_order(blocks.swapaxes(0, 1).reshape(-1, *value.shape), dim)


def sum_in_order(blocks, axes, order):
    inside = blocks.shape[1:]
    blocks = blocks.reshape(*(lax.axis_size(a) for a in axes), *inside)
    blocks = jnp.moveaxis(blocks, order, range(len(axes))).reshape(-1, *inside)
    for k in order:
        blocks = lax.psum_scatter(blocks, axes[k], scatter_dimension=0, tiled=True)
    return blocks[0]


def in_blocks(value, dim, length):
    before, after = (value.shape[:dim], value.shape[dim + 1 :])
    return jnp.moveaxis(value.reshape(*before, length, -1, *after), dim, 0)


def sum_by_axis(value, axes, order, dim):
    length = lax.axis_size(axes)
    return sum_in_order(in_blocks(value, dim, length), axes, order)


def by_axis(value, axes):
    for axis in axes:
        value = lax.psum(value, axis)
    return value


def lookup(steps, table):
    match = steps[:, None] == jnp.arange(table.shape[0], dtype=jnp.int32)[None, :]
    return jnp.sum(jnp.where(match, table[None, :], jnp.zeros((), table.dtype)), axis=1)


def layer_norm(values, gain):
    wide = values.astype(jnp.float32)
    center = wide - jnp.mean(wide, axis=-1, keepdims=True)
    spread = jnp.mean(center * center, axis=-1, keepdims=True)
    return (center * lax.rsqrt(spread + 1e-05) * gain).astype(jnp.bfloat16)


def make_adder(flat, piece):
    return jnp.einsum("rn,tnc->trc", flat, piece, preferred_element_type=jnp.float32)


def attend(operands):
    query_one, keys_one, values_one = operands
    rows = query_one.shape[0]
    total = keys_one.shape[0]
    scores = jnp.einsum(
        "qhd,khd->hqk",
        query_one.reshape(rows, HEADS, HEAD),
        keys_one.reshape(total, HEADS, HEAD),
        preferred_element_type=jnp.float32,
    ) * HEAD ** (-0.5)
    probs = jax.nn.softmax(scores, axis=-1).astype(jnp.bfloat16)
    mixed = jnp.einsum(
        "hqk,khd->qhd",
        probs,
        values_one.reshape(total, HEADS, HEAD),
        preferred_element_type=jnp.float32,
    )
    return mixed.astype(jnp.bfloat16).reshape(rows, D)


def shards(
    clean,
    noise,
    tsteps,
    alpha_tab,
    weight_tab,
    norm1_gain,
    norm2_gain,
    wqkv,
    wout,
    wgate,
    wvalue,
    wdown,
):
    samples, local_rows, width = clean.shape
    alpha = lookup(tsteps, alpha_tab)
    sigma = jnp.sqrt(1.0 - alpha * alpha)
    weight = lookup(tsteps, weight_tab)
    noised = (
        alpha[:, None, None] * clean.astype(jnp.float32)
        + sigma[:, None, None] * noise.astype(jnp.float32)
    ).astype(jnp.bfloat16)
    normed1 = layer_norm(noised, norm1_gain)
    full_cols = gathered_copies(wqkv, MP, 2)
    flat = normed1.reshape(samples * local_rows, width)
    projected = make_adder(flat, lax.all_gather(full_cols, DP, axis=1, tiled=True)).astype(
        jnp.bfloat16
    )
    query = projected[0].reshape(samples, local_rows, width)
    keys_part = projected[1].reshape(samples, local_rows, width)
    values_part = projected[2].reshape(samples, local_rows, width)
    keys_all, values_all = sent_together((keys_part, values_part), MP, 1, 0)
    mixed = lax.map(attend, (query, keys_all, values_all))
    mixed_flat = mixed.reshape(samples * local_rows, width)
    out_cols = gathered_copies(wout, MP, 1)
    part = mixed_flat
    projected_out = jnp.dot(
        part, whole_of(out_cols, (("dp_0", "dp_1"), "dp_2"), 0), preferred_element_type=jnp.float32
    )
    resid = (noised.astype(jnp.float32) + projected_out.reshape(samples, local_rows, width)).astype(
        jnp.bfloat16
    )
    normed2 = layer_norm(resid, norm2_gain)
    ff_in = lax.all_gather(normed2, MP, axis=1, tiled=True)
    all_rows = ff_in.shape[1]
    ff_flat = ff_in.reshape(samples * all_rows, width)
    pieces = sent_together((wgate, wvalue), DP, 0, 1)
    part = ff_flat
    gate = jnp.dot(part, pieces[0], preferred_element_type=jnp.float32)
    value = jnp.dot(part, pieces[1], preferred_element_type=jnp.float32)
    hidden = (jax.nn.gelu(gate, approximate=False) * value).astype(jnp.bfloat16)
    block_sum = jnp.dot(
        hidden, whole_of(wdown, (("dp_0", "dp_1"), "dp_2"), 1), preferred_element_type=jnp.float32
    )
    ff_out = sum_by_axis(
        block_sum.reshape(samples, all_rows, width).astype(jnp.bfloat16), MP, (1, 0), 1
    ).astype(jnp.float32)
    prediction = resid.astype(jnp.float32) + ff_out
    denoised = (noised.astype(jnp.float32) - sigma[:, None, None] * prediction) / alpha[
        :, None, None
    ]
    error = denoised - clean.astype(jnp.float32)
    local_terms = jnp.sum(weight * jnp.sum(error * error, axis=(1, 2))) / (L * D)
    loss = by_axis(local_terms, DP_MP)
    return (denoised, loss)


def solution(mesh):
    split = Mesh(mesh.devices.reshape(4, 4, 2, 2, 4), ("dp_0", "dp_1", "dp_2", "mp_0", "mp_1"))
    in_specs = (
        P(DP, MP, None),
        P(DP, MP, None),
        P(DP),
        P(),
        P(),
        P(),
        P(),
        P(None, DP, MP),
        P(DP, MP),
        P(DP, MP),
        P(DP, MP),
        P(MP, DP),
    )
    out_specs = (P(DP, MP, None), P())
    return jax.shard_map(
        shards, mesh=split, in_specs=in_specs, out_specs=out_specs, check_vma=False
    )
```

profile of v0, /device:TPU:32, one launch (start us, length us, event | category | flops | bytes accessed | tf_op | source)
XLA Modules:
  0.0 535.7 jit_solution(18051994592071202623)
XLA Ops:
  7.3 0.9 broadcast_in_dim.27
  8.2 28.9 %all_to_all.30 = bf16[8,3,40,160]{3,2,1,0:T(8,128)(2,1)S(1)} all-to-all(bf16[8,3,40,160]{3,2,1,0:T(8,128)(2,1)S(1)} %broadcast_in_dim.27), channel_id=1, replica_groups=mesh['dp_0'=4,'dp_1'=4,'dp_2'=2,'mp_0'=2,'mp_1'=4] {'mp_0','mp_1'}, dimensions={0} | all-to-all | bytes 614400 | tf_op jit(solution)/shard_map/all_to_all | solution.py:18
  37.2 1.2 reshape.152
  42.0 62.0 %all-gather.5.cloned.1.call-done = bf16[3,1280,1280]{2,1,0:T(8,128)(2,1)} async-done(((bf16[3,40,1280]{2,1,0:T(8,128)(2,1)}), bf16[3,1280,1280]{2,1,0:T(8,128)(2,1)}) %all-gather.5.cloned.1.call-update) | async-done | bytes 9830416 | tf_op jit(solution)/shard_map/all_gather | solution.py:135
  104.0 5.3 fusion.21
  110.2 20.1 %all_to_all.31 = bf16[8,40,160]{2,1,0:T(8,128)(2,1)S(1)} all-to-all(bf16[8,40,160]{2,1,0:T(8,128)(2,1)S(1)} %broadcast_in_dim.28), channel_id=1, replica_groups=mesh['dp_0'=4,'dp_1'=4,'dp_2'=2,'mp_0'=2,'mp_1'=4] {'mp_0','mp_1'}, dimensions={0} | all-to-all | bytes 204800 | tf_op jit(solution)/shard_map/all_to_all | solution.py:18
  130.6 1.3 broadcast_in_dim.30
  131.9 5.5 %all-to-all-start.2 = ((bf16[16,40,1280]{2,1,0:T(8,128)(2,1)}), bf16[16,40,1280]{2,1,0:T(8,128)(2,1)S(1)}, u32[]{:S(2)}, u32[]{:S(2)}) async-start(bf16[16,40,1280]{2,1,0:T(8,128)(2,1)} %broadcast_in_dim.30), calls=%async_computation.2 | async-start | bytes 3276800 | tf_op jit(solution)/shard_map/all_to_all | solution.py:18
  138.2 94.0 %all-to-all-done.2 = bf16[16,40,1280]{2,1,0:T(8,128)(2,1)S(1)} async-done(((bf16[16,40,1280]{2,1,0:T(8,128)(2,1)}), bf16[16,40,1280]{2,1,0:T(8,128)(2,1)S(1)}, u32[]{:S(2)}, u32[]{:S(2)}) %all-to-all-start.2) | async-done | bytes 1638432 | tf_op jit(solution)/shard_map/all_to_all | solution.py:18
  232.4 6.4 %all_to_all.32 = bf16[2,16,40,1280]{3,2,1,0:T(8,128)(2,1)S(1)} all-to-all(bf16[2,16,40,1280]{3,2,1,0:T(8,128)(2,1)S(1)} %broadcast_in_dim.31), channel_id=1, replica_groups=mesh['dp_0'=4,'dp_1'=4,'dp_2'=2,'mp_0'=2,'mp_1'=4] {'dp_2'}, dimensions={0} | all-to-all | bytes 6553600 | tf_op jit(solution)/shard_map/all_to_all | solution.py:18
  238.8 1.9 copy.28
  240.7 0.9 copy.25
  241.6 4.4 fusion.88
  246.0 4.5 copy.24
  250.5 2.7 copy.26
  253.2 9.2 %fusion.89 = (f32[20,128]{1,0:T(8,128)S(1)}, f32[20,128,1024]{2,1,0:T(8,128)}) fusion(bf16[128,20,64]{0,2,1:T(8,128)(2,1)} %bitcast.72, bf16[1024,20,64]{0,2,1:T(8,128)(2,1)} %bitcast.66), kind=kOutput, calls=%fused_computation.105 | convolution fusion | flops 343409664 | bytes 13445120 | tf_op jit(solution)/shard_map/while/body/eval_jaxpr/sub | solution.py:100
  262.4 6.2 %fusion.28 = bf16[20,64,128]{2,1,0:T(8,128)(2,1)S(1)} fusion(bf16[1024,20,64]{0,2,1:T(8,128)(2,1)S(1)} %bitcast.65, f32[20,128,1024]{2,1,0:T(8,128)} %get-tuple-element.24, f32[20,128]{1,0:T(8,128)S(1)} %get-tuple-element.23), kind=kOutput, calls=%fused_computation.40 | convolution fusion | flops 340951040 | bytes 13445120 | tf_op jit(solution)/shard_map/while/body/eval_jaxpr/hqk,khd->qhd/dot_general | solution.py:101
  269.7 0.9 multiply_convert_fusion
  270.7 30.8 %all_to_all.33 = bf16[16,640,40]{1,2,0:T(8,128)(2,1)S(1)} all-to-all(bf16[16,640,40]{1,2,0:T(8,128)(2,1)S(1)} %broadcast_in_dim.32), channel_id=1, replica_groups=mesh['dp_0'=4,'dp_1'=4,'dp_2'=2,'mp_0'=2,'mp_1'=4] {'dp_0','dp_1'}, dimensions={0} | all-to-all | bytes 1638400 | tf_op jit(solution)/shard_map/all_to_all | solution.py:18
  301.6 5.1 all_to_all.34
  306.8 83.4 %all-gather.9.cloned.1.call-done = bf16[1,1024,1280]{2,1,0:T(8,128)(2,1)} async-done(((bf16[1,128,1280]{2,1,0:T(8,128)(2,1)}), bf16[1,1024,1280]{2,1,0:T(8,128)(2,1)}) %all-gather.9.cloned.1.call-update) | async-done | bytes 2621456 | tf_op jit(solution)/shard_map/all_gather | solution.py:153
  390.2 5.9 %fusion.10 = f32[1024,640]{1,0:T(8,128)} fusion(bf16[1,1024,1280]{2,1,0:T(8,128)(2,1)} %all-gather.9.cloned.1.call-done, bf16[1280,1280]{1,0:T(8,128)(2,1)} %all-gather.11.cloned.1.call-done), kind=kOutput, calls=%fused_computation.14 | convolution fusion | flops 1677721600 | bytes 6881280 | tf_op jit(solution)/shard_map/dot_general | solution.py:159
  396.2 12.9 %convolution_convert_fusion = bf16[1024,1280]{1,0:T(8,128)(2,1)} fusion(bf16[640,1280]{0,1:T(8,128)(2,1)S(1)} %bitcast.69, f32[1024,640]{1,0:T(8,128)} %fusion.10, bf16[1,1024,1280]{2,1,0:T(8,128)(2,1)} %all-gather.9.cloned.1.call-done, bf16[1280,1280]{1,0:T(8,128)(2,1)} %all-gather.11.cloned.1.call-done), kind=kOutput, calls=%fused_computation.8 | convolution fusion | flops 3400007680 | bytes 11141120 | tf_op jit(solution)/shard_map/dot_general | solution.py:161
  409.1 3.4 copy.30
  412.6 33.2 %reduce-scatter.3.cloned.1.call-done = bf16[2,1,128,1280]{3,2,1,0:T(8,128)(2,1)} async-done(((bf16[8,1,128,1280]{3,2,1,0:T(8,128)(2,1)}), bf16[2,1,128,1280]{3,2,1,0:T(8,128)(2,1)}) %reduce-scatter.3.cloned.1.call-update) | async-done | bytes 655376 | tf_op jit(solution)/shard_map/reduce_scatter | solution.py:54
  446.5 33.0 %reduce-scatter.5.cloned.1.call-done = bf16[1,1,128,1280]{3,2,1,0:T(8,128)(2,1)} async-done(((bf16[2,1,128,1280]{3,2,1,0:T(8,128)(2,1)}), bf16[1,1,128,1280]{3,2,1,0:T(8,128)(2,1)}) %reduce-scatter.5.cloned.1.call-update) | async-done | bytes 327696 | tf_op jit(solution)/shard_map/reduce_scatter | solution.py:54
  479.5 3.2 fusion.47
  484.0 10.2 %psum.35 = f32[]{:T(128)} all-reduce(f32[]{:T(128)S(6)} %div.40), channel_id=1, replica_groups=mesh['dp_0'=4,'dp_1'=4,'dp_2'=2,'mp_0'=2,'mp_1'=4] {'dp_0'}, use_global_device_ids=true, to_apply=%region_11.12 | all-reduce | flops 1 | bytes 8 | tf_op jit(solution)/shard_map/psum | solution.py:70
  494.2 11.1 %psum.36 = f32[]{:T(128)} all-reduce(f32[]{:T(128)} %psum.35), channel_id=1, replica_groups=mesh['dp_0'=4,'dp_1'=4,'dp_2'=2,'mp_0'=2,'mp_1'=4] {'dp_1'}, use_global_device_ids=true, to_apply=%region_12.13 | all-reduce | flops 1 | bytes 8 | tf_op jit(solution)/shard_map/psum | solution.py:70
  505.2 3.1 psum.37
  508.3 9.4 %psum.38 = f32[]{:T(128)} all-reduce(f32[]{:T(128)} %psum.37), channel_id=1, replica_groups=mesh['dp_0'=4,'dp_1'=4,'dp_2'=2,'mp_0'=2,'mp_1'=4] {'mp_0'}, use_global_device_ids=true, to_apply=%region_14.15 | all-reduce | flops 1 | bytes 8 | tf_op jit(solution)/shard_map/psum | solution.py:70
  517.8 11.1 %psum.39 = f32[]{:T(128)} all-reduce(f32[]{:T(128)} %psum.38), channel_id=1, replica_groups=mesh['dp_0'=4,'dp_1'=4,'dp_2'=2,'mp_0'=2,'mp_1'=4] {'mp_1'}, use_global_device_ids=true, to_apply=%region_15.16 | all-reduce | flops 1 | bytes 8 | tf_op jit(solution)/shard_map/psum | solution.py:70
  (59 shorter events, 6.1 us)
Async XLA Ops:
  7.2 31.9 %copy-start.10 = (f32[1000]{0:T(1024)S(1)}, f32[1000]{0:T(1024)}, u32[]{:S(2)}) copy-start(f32[1000]{0:T(1024)} %param.15) | copy-start | bytes 12004
  7.2 33.7 %copy-start.2 = (bf16[1,128,1280]{2,1,0:T(8,128)(2,1)S(1)}, bf16[1,128,1280]{2,1,0:T(8,128)(2,1)}, u32[]{:S(2)}) copy-start(bf16[1,128,1280]{2,1,0:T(8,128)(2,1)} %param.12) | copy-start | bytes 983044
  7.2 33.7 %copy-start.3 = (bf16[1,128,1280]{2,1,0:T(8,128)(2,1)S(1)}, bf16[1,128,1280]{2,1,0:T(8,128)(2,1)}, u32[]{:S(2)}) copy-start(bf16[1,128,1280]{2,1,0:T(8,128)(2,1)} %param.13) | copy-start | bytes 983044
  7.2 96.8 %copy-start.8 = (f32[1280]{0:T(1024)S(1)}, f32[1280]{0:T(1024)}, u32[]{:S(2)}) copy-start(f32[1280]{0:T(1024)} %param.17) | copy-start | bytes 15364
  7.2 96.8 %all-gather.5.cloned.1.call-start = ((), (), s32[]{:S(2)}) async-start(), calls=%async_computation.8 | async-start | bytes 10137600 | tf_op jit(solution)/shard_map/all_gather | solution.py:135
  38.4 203.2 %all-gather.7.cloned.1.call-start = ((), (), s32[]{:S(2)}) async-start(), calls=%async_computation.9 | async-start | bytes 5898240 | tf_op jit(solution)/shard_map/all_gather | solution.py:40
  42.0 68.3 %copy-start.7 = (bf16[40,160]{1,0:T(8,128)(2,1)S(1)}, bf16[40,160]{1,0:T(8,128)(2,1)}, u32[]{:S(2)}) copy-start(bf16[40,160]{1,0:T(8,128)(2,1)} %param.20) | copy-start | bytes 38404
  130.4 7.1 %copy-start.4 = (bf16[40,640]{1,0:T(8,128)(2,1)S(1)}, bf16[40,640]{1,0:T(8,128)(2,1)}, u32[]{:S(2)}) copy-start(bf16[40,640]{1,0:T(8,128)(2,1)} %param.22) | copy-start | bytes 153604
  130.4 7.1 %copy-start.5 = (bf16[40,640]{1,0:T(8,128)(2,1)S(1)}, bf16[40,640]{1,0:T(8,128)(2,1)}, u32[]{:S(2)}) copy-start(bf16[40,640]{1,0:T(8,128)(2,1)} %param.21) | copy-start | bytes 153604
  131.9 100.3 %all-to-all-start.2 = ((bf16[16,40,1280]{2,1,0:T(8,128)(2,1)}), bf16[16,40,1280]{2,1,0:T(8,128)(2,1)S(1)}, u32[]{:S(2)}, u32[]{:S(2)}) async-start(bf16[16,40,1280]{2,1,0:T(8,128)(2,1)} %broadcast_in_dim.30), calls=%async_computation.2 | async-start | bytes 3276800 | tf_op jit(solution)/shard_map/all_to_all | solution.py:18
  137.4 169.4 %all-gather.11.cloned.1.call-start = ((), (), s32[]{:S(2)}) async-start(), calls=%async_computation.11 | async-start | bytes 3379200 | tf_op jit(solution)/shard_map/all_gather | solution.py:40
  138.2 252.1 %all-gather.9.cloned.1.call-start = ((), (), s32[]{:S(2)}) async-start(), calls=%async_computation.10 | async-start | bytes 2949120 | tf_op jit(solution)/shard_map/all_gather | solution.py:153
  253.2 9.2 %copy-start.1 = (bf16[1,1024,1280]{1,2,0:T(8,128)(2,1)S(1)}, bf16[1,1024,1280]{1,2,0:T(8,128)(2,1)}, u32[]{:S(2)}) copy-start(bf16[1,1024,1280]{1,2,0:T(8,128)(2,1)} %copy.24) | copy-start | bytes 7864324
  262.4 6.2 %copy-start = (bf16[2,16,40,1280]{3,2,0,1:T(8,128)(2,1)S(1)}, bf16[2,16,40,1280]{3,2,0,1:T(8,128)(2,1)}, u32[]{:S(2)}) copy-start(bf16[2,16,40,1280]{3,2,0,1:T(8,128)(2,1)} %copy.28) | copy-start | bytes 9830404
  268.6 1.0 copy-start.9
  268.7 2.0 copy-start.6
  270.6 175.2 %reduce-scatter.3.cloned.1.call-start = ((), (), s32[]{:S(2)}) async-start(), calls=%async_computation.12 | async-start | bytes 3276800 | tf_op jit(solution)/shard_map/reduce_scatter | solution.py:54
  412.5 33.3 %copy-start.11 = (f32[1000]{0:T(1024)S(1)}, f32[1000]{0:T(1024)}, u32[]{:S(2)}) copy-start(f32[1000]{0:T(1024)} %param.16) | copy-start | bytes 12004
  412.5 67.0 %reduce-scatter.5.cloned.1.call-start = ((), (), s32[]{:S(2)}) async-start(), calls=%async_computation.13 | async-start | bytes 983040 | tf_op jit(solution)/shard_map/reduce_scatter | solution.py:54
Sparse Core Ops, SparseCore 0:
  38.5 65.4 all-gather.4
  110.3 98.7 all-gather.6
  211.0 93.0 all-gather.10
  307.1 83.1 all-gather.8
  412.6 33.1 reduce-scatter.2
  448.1 31.2 reduce-scatter.4
where the time goes:
time: 536 us
  waiting for transfers between devices  306 us (57%)
  blocking collectives  136 us (25%)
  matrix products  40.3 us (8%)
  local copies, waits for them, and re-layouts  23.1 us (4%)
  between operations  17.5 us (3%)
  other arithmetic  7.28 us (1%)
  starting transfers between devices  5.74 us (1%)
    all_to_all x1, waiting for transfers between devices, copy_for_each(): lax.all_to_all(jnp.broadcast_to(value[None], (length, *value.shape)), axi...  94 us
    all_to_all x5, blocking collectives, copy_for_each(): lax.all_to_all(jnp.broadcast_to(value[None], (length, *value.shape)), axi...  91.2 us
    all_gather x1, waiting for transfers between devices, shards(): ff_in = lax.all_gather(normed2, MP, axis=1, tiled=True)  83.4 us
    reduce_scatter x2, waiting for transfers between devices, sum_in_order(): blocks = lax.psum_scatter(blocks, axes[k], scatter_dimension=0, tiled=True)  66.2 us
    all_gather x1, waiting for transfers between devices, shards(): lax.all_gather(full_cols, DP, axis=1, tiled=True)  62 us
    psum x5, blocking collectives, by_axis(): value = lax.psum(value, axis)  44.8 us
    dot_general x1, matrix products, shards(): jnp.dot(hidden, whole_of(wdown, (('dp_0', 'dp_1'), 'dp_2'), 1), preferred...  12.9 us
    split x3, local copies, waits for them, and re-layouts, sent_together(): jnp.split(lax.all_gather(both, axis, axis=dim, tiled=True), ends, axis=al...  11.6 us
  transfers between devices with their start and end apart: 7, of which 5 were waited for; matrix products, arithmetic and copies ran while one was open for 7% of the time, Pallas kernels for 0%

commit v1 on v0

--- a/solution.py
+++ b/solution.py
@@ -150,7 +150,7 @@
         jnp.bfloat16
     )
     normed2 = layer_norm(resid, norm2_gain)
-    ff_in = lax.all_gather(normed2, MP, axis=1, tiled=True)
+    ff_in = jnp.concatenate(lax.all_gather(normed2, MP), axis=1)
     all_rows = ff_in.shape[1]
     ff_flat = ff_in.reshape(samples * all_rows, width)
     pieces = sent_together((wgate, wvalue), DP, 0, 1)

time: 536 us -> 536 us (level)
  no operation moved by 1% of the time
where the time goes in v1:
time: 536 us; the launch traced here: 535 us
  waiting for transfers between devices  306 us (57%)
  blocking collectives  136 us (25%)
  matrix products  40 us (7%)
  local copies, waits for them, and re-layouts  23.1 us (4%)
  between operations  17.5 us (3%)
  other arithmetic  7.28 us (1%)
  starting transfers between devices  5.74 us (1%)
    all_to_all x1, waiting for transfers between devices, copy_for_each(): lax.all_to_all(jnp.broadcast_to(value[None], (length, *value.shape)), axi...  94 us
    all_to_all x5, blocking collectives, copy_for_each(): lax.all_to_all(jnp.broadcast_to(value[None], (length, *value.shape)), axi...  91.2 us
    all_gather x1, waiting for transfers between devices, shards(): ff_in = jnp.concatenate(lax.all_gather(normed2, MP), axis=1)  83.4 us
    reduce_scatter x2, waiting for transfers between devices, sum_in_order(): blocks = lax.psum_scatter(blocks, axes[k], scatter_dimension=0, tiled=True)  66.2 us
    all_gather x1, waiting for transfers between devices, shards(): lax.all_gather(full_cols, DP, axis=1, tiled=True)  62 us
    psum x5, blocking collectives, by_axis(): value = lax.psum(value, axis)  44.8 us
    dot_general x1, matrix products, shards(): jnp.dot(hidden, whole_of(wdown, (('dp_0', 'dp_1'), 'dp_2'), 1), preferred...  12.6 us
    split x3, local copies, waits for them, and re-layouts, sent_together(): jnp.split(lax.all_gather(both, axis, axis=dim, tiled=True), ends, axis=al...  11.6 us
  transfers between devices with their start and end apart: 7, of which 5 were waited for; matrix products, arithmetic and copies ran while one was open for 7% of the time, Pallas kernels for 0%

profile of v1, /device:TPU:32, one launch (start us, length us, event | category | flops | bytes accessed | tf_op | source)
XLA Modules:
  0.0 535.4 jit_solution(9544459507857209948)
XLA Ops:
  7.3 0.9 broadcast_in_dim.27
  8.2 28.9 %all_to_all.30 = bf16[8,3,40,160]{3,2,1,0:T(8,128)(2,1)S(1)} all-to-all(bf16[8,3,40,160]{3,2,1,0:T(8,128)(2,1)S(1)} %broadcast_in_dim.27), channel_id=1, replica_groups=mesh['dp_0'=4,'dp_1'=4,'dp_2'=2,'mp_0'=2,'mp_1'=4] {'mp_0','mp_1'}, dimensions={0} | all-to-all | bytes 614400 | tf_op jit(solution)/shard_map/all_to_all | solution.py:18
  37.2 1.2 reshape.149
  42.0 62.0 %all-gather.6.cloned.1.call-done = bf16[3,1280,1280]{2,1,0:T(8,128)(2,1)} async-done(((bf16[3,40,1280]{2,1,0:T(8,128)(2,1)}), bf16[3,1280,1280]{2,1,0:T(8,128)(2,1)}) %all-gather.6.cloned.1.call-update) | async-done | bytes 9830416 | tf_op jit(solution)/shard_map/all_gather | solution.py:135
  104.0 5.3 fusion.17
  110.2 20.1 %all_to_all.31 = bf16[8,40,160]{2,1,0:T(8,128)(2,1)S(1)} all-to-all(bf16[8,40,160]{2,1,0:T(8,128)(2,1)S(1)} %broadcast_in_dim.28), channel_id=1, replica_groups=mesh['dp_0'=4,'dp_1'=4,'dp_2'=2,'mp_0'=2,'mp_1'=4] {'mp_0','mp_1'}, dimensions={0} | all-to-all | bytes 204800 | tf_op jit(solution)/shard_map/all_to_all | solution.py:18
  130.6 1.3 broadcast_in_dim.30
  131.9 5.5 %all-to-all-start.2 = ((bf16[16,40,1280]{2,1,0:T(8,128)(2,1)}), bf16[16,40,1280]{2,1,0:T(8,128)(2,1)S(1)}, u32[]{:S(2)}, u32[]{:S(2)}) async-start(bf16[16,40,1280]{2,1,0:T(8,128)(2,1)} %broadcast_in_dim.30), calls=%async_computation.2 | async-start | bytes 3276800 | tf_op jit(solution)/shard_map/all_to_all | solution.py:18
  138.2 94.0 %all-to-all-done.2 = bf16[16,40,1280]{2,1,0:T(8,128)(2,1)S(1)} async-done(((bf16[16,40,1280]{2,1,0:T(8,128)(2,1)}), bf16[16,40,1280]{2,1,0:T(8,128)(2,1)S(1)}, u32[]{:S(2)}, u32[]{:S(2)}) %all-to-all-start.2) | async-done | bytes 1638432 | tf_op jit(solution)/shard_map/all_to_all | solution.py:18
  232.4 6.4 %all_to_all.32 = bf16[2,16,40,1280]{3,2,1,0:T(8,128)(2,1)S(1)} all-to-all(bf16[2,16,40,1280]{3,2,1,0:T(8,128)(2,1)S(1)} %broadcast_in_dim.31), channel_id=1, replica_groups=mesh['dp_0'=4,'dp_1'=4,'dp_2'=2,'mp_0'=2,'mp_1'=4] {'dp_2'}, dimensions={0} | all-to-all | bytes 6553600 | tf_op jit(solution)/shard_map/all_to_all | solution.py:18
  238.8 1.9 copy.28
  240.7 0.9 copy.25
  241.6 4.4 fusion.78
  246.0 4.5 copy.24
  250.5 2.7 copy.26
  253.2 9.2 %fusion.79 = (f32[20,128]{1,0:T(8,128)S(1)}, f32[20,128,1024]{2,1,0:T(8,128)}) fusion(bf16[128,20,64]{0,2,1:T(8,128)(2,1)} %bitcast.66, bf16[1024,20,64]{0,2,1:T(8,128)(2,1)} %bitcast.60), kind=kOutput, calls=%fused_computation.102 | convolution fusion | flops 343409664 | bytes 13445120 | tf_op jit(solution)/shard_map/while/body/eval_jaxpr/sub | solution.py:100
  262.4 6.2 %fusion.26 = bf16[20,64,128]{2,1,0:T(8,128)(2,1)S(1)} fusion(bf16[1024,20,64]{0,2,1:T(8,128)(2,1)S(1)} %bitcast.59, f32[20,128,1024]{2,1,0:T(8,128)} %get-tuple-element.24, f32[20,128]{1,0:T(8,128)S(1)} %get-tuple-element.23), kind=kOutput, calls=%fused_computation.37 | convolution fusion | flops 340951040 | bytes 13445120 | tf_op jit(solution)/shard_map/while/body/eval_jaxpr/hqk,khd->qhd/dot_general | solution.py:101
  269.7 0.9 multiply_convert_fusion
  270.7 30.8 %all_to_all.33 = bf16[16,640,40]{1,2,0:T(8,128)(2,1)S(1)} all-to-all(bf16[16,640,40]{1,2,0:T(8,128)(2,1)S(1)} %broadcast_in_dim.32), channel_id=1, replica_groups=mesh['dp_0'=4,'dp_1'=4,'dp_2'=2,'mp_0'=2,'mp_1'=4] {'dp_0','dp_1'}, dimensions={0} | all-to-all | bytes 1638400 | tf_op jit(solution)/shard_map/all_to_all | solution.py:18
  301.6 5.1 all_to_all.34
  306.8 83.4 %all-gather.12.cloned.1.call-done = bf16[8,128,1280]{2,1,0:T(8,128)(2,1)} async-done(((bf16[1,128,1280]{2,1,0:T(8,128)(2,1)}), bf16[8,128,1280]{2,1,0:T(8,128)(2,1)}) %all-gather.12.cloned.1.call-update) | async-done | bytes 2621456 | tf_op jit(solution)/shard_map/all_gather | solution.py:153
  390.2 5.9 %fusion.22 = f32[1024,640]{1,0:T(8,128)} fusion(bf16[1024,1280]{1,0:T(8,128)(2,1)} %bitcast.67, bf16[1280,1280]{1,0:T(8,128)(2,1)} %all-gather.10.cloned.1.call-done), kind=kOutput, calls=%fused_computation.35 | convolution fusion | flops 1677721600 | bytes 6881280 | tf_op jit(solution)/shard_map/dot_general | solution.py:158
  396.2 12.6 %convolution_convert_fusion = bf16[1024,1280]{1,0:T(8,128)(2,1)} fusion(bf16[640,1280]{0,1:T(8,128)(2,1)S(1)} %bitcast.63, f32[1024,640]{1,0:T(8,128)} %fusion.22, bf16[1024,1280]{1,0:T(8,128)(2,1)} %bitcast.68, bf16[1280,1280]{1,0:T(8,128)(2,1)} %all-gather.10.cloned.1.call-done), kind=kOutput, calls=%fused_computation.8 | convolution fusion | flops 3400007680 | bytes 11141120 | tf_op jit(solution)/shard_map/dot_general | solution.py:161
  408.7 3.4 copy.30
  412.2 33.2 %reduce-scatter.3.cloned.1.call-done = bf16[2,1,128,1280]{3,2,1,0:T(8,128)(2,1)} async-done(((bf16[8,1,128,1280]{3,2,1,0:T(8,128)(2,1)}), bf16[2,1,128,1280]{3,2,1,0:T(8,128)(2,1)}) %reduce-scatter.3.cloned.1.call-update) | async-done | bytes 655376 | tf_op jit(solution)/shard_map/reduce_scatter | solution.py:54
  446.2 33.0 %reduce-scatter.5.cloned.1.call-done = bf16[1,1,128,1280]{3,2,1,0:T(8,128)(2,1)} async-done(((bf16[2,1,128,1280]{3,2,1,0:T(8,128)(2,1)}), bf16[1,1,128,1280]{3,2,1,0:T(8,128)(2,1)}) %reduce-scatter.5.cloned.1.call-update) | async-done | bytes 327696 | tf_op jit(solution)/shard_map/reduce_scatter | solution.py:54
  479.1 3.2 fusion.37
  483.7 10.2 %psum.35 = f32[]{:T(128)} all-reduce(f32[]{:T(128)S(6)} %div.40), channel_id=1, replica_groups=mesh['dp_0'=4,'dp_1'=4,'dp_2'=2,'mp_0'=2,'mp_1'=4] {'dp_0'}, use_global_device_ids=true, to_apply=%region_11.12 | all-reduce | flops 1 | bytes 8 | tf_op jit(solution)/shard_map/psum | solution.py:70
  493.9 11.0 %psum.36 = f32[]{:T(128)} all-reduce(f32[]{:T(128)} %psum.35), channel_id=1, replica_groups=mesh['dp_0'=4,'dp_1'=4,'dp_2'=2,'mp_0'=2,'mp_1'=4] {'dp_1'}, use_global_device_ids=true, to_apply=%region_12.13 | all-reduce | flops 1 | bytes 8 | tf_op jit(solution)/shard_map/psum | solution.py:70
  504.9 3.1 psum.37
  508.0 9.4 %psum.38 = f32[]{:T(128)} all-reduce(f32[]{:T(128)} %psum.37), channel_id=1, replica_groups=mesh['dp_0'=4,'dp_1'=4,'dp_2'=2,'mp_0'=2,'mp_1'=4] {'mp_0'}, use_global_device_ids=true, to_apply=%region_14.15 | all-reduce | flops 1 | bytes 8 | tf_op jit(solution)/shard_map/psum | solution.py:70
  517.4 11.1 %psum.39 = f32[]{:T(128)} all-reduce(f32[]{:T(128)} %psum.38), channel_id=1, replica_groups=mesh['dp_0'=4,'dp_1'=4,'dp_2'=2,'mp_0'=2,'mp_1'=4] {'mp_1'}, use_global_device_ids=true, to_apply=%region_15.16 | all-reduce | flops 1 | bytes 8 | tf_op jit(solution)/shard_map/psum | solution.py:70
  (59 shorter events, 6.1 us)
Async XLA Ops:
  7.2 31.9 %copy-start.10 = (f32[1000]{0:T(1024)S(1)}, f32[1000]{0:T(1024)}, u32[]{:S(2)}) copy-start(f32[1000]{0:T(1024)} %param.15) | copy-start | bytes 12004
  7.2 33.7 %copy-start.2 = (bf16[1,128,1280]{2,1,0:T(8,128)(2,1)S(1)}, bf16[1,128,1280]{2,1,0:T(8,128)(2,1)}, u32[]{:S(2)}) copy-start(bf16[1,128,1280]{2,1,0:T(8,128)(2,1)} %param.12) | copy-start | bytes 983044
  7.2 33.7 %copy-start.3 = (bf16[1,128,1280]{2,1,0:T(8,128)(2,1)S(1)}, bf16[1,128,1280]{2,1,0:T(8,128)(2,1)}, u32[]{:S(2)}) copy-start(bf16[1,128,1280]{2,1,0:T(8,128)(2,1)} %param.13) | copy-start | bytes 983044
  7.2 96.8 %copy-start.8 = (f32[1280]{0:T(1024)S(1)}, f32[1280]{0:T(1024)}, u32[]{:S(2)}) copy-start(f32[1280]{0:T(1024)} %param.17) | copy-start | bytes 15364
  7.2 96.8 %all-gather.6.cloned.1.call-start = ((), (), s32[]{:S(2)}) async-start(), calls=%async_computation.8 | async-start | bytes 10137600 | tf_op jit(solution)/shard_map/all_gather | solution.py:135
  38.4 203.2 %all-gather.8.cloned.1.call-start = ((), (), s32[]{:S(2)}) async-start(), calls=%async_computation.9 | async-start | bytes 5898240 | tf_op jit(solution)/shard_map/all_gather | solution.py:40
  42.0 68.3 %copy-start.7 = (bf16[40,160]{1,0:T(8,128)(2,1)S(1)}, bf16[40,160]{1,0:T(8,128)(2,1)}, u32[]{:S(2)}) copy-start(bf16[40,160]{1,0:T(8,128)(2,1)} %param.20) | copy-start | bytes 38404
  130.4 7.1 %copy-start.4 = (bf16[40,640]{1,0:T(8,128)(2,1)S(1)}, bf16[40,640]{1,0:T(8,128)(2,1)}, u32[]{:S(2)}) copy-start(bf16[40,640]{1,0:T(8,128)(2,1)} %param.22) | copy-start | bytes 153604
  130.4 7.1 %copy-start.5 = (bf16[40,640]{1,0:T(8,128)(2,1)S(1)}, bf16[40,640]{1,0:T(8,128)(2,1)}, u32[]{:S(2)}) copy-start(bf16[40,640]{1,0:T(8,128)(2,1)} %param.21) | copy-start | bytes 153604
  131.9 100.3 %all-to-all-start.2 = ((bf16[16,40,1280]{2,1,0:T(8,128)(2,1)}), bf16[16,40,1280]{2,1,0:T(8,128)(2,1)S(1)}, u32[]{:S(2)}, u32[]{:S(2)}) async-start(bf16[16,40,1280]{2,1,0:T(8,128)(2,1)} %broadcast_in_dim.30), calls=%async_computation.2 | async-start | bytes 3276800 | tf_op jit(solution)/shard_map/all_to_all | solution.py:18
  137.4 169.4 %all-gather.10.cloned.1.call-start = ((), (), s32[]{:S(2)}) async-start(), calls=%async_computation.10 | async-start | bytes 3379200 | tf_op jit(solution)/shard_map/all_gather | solution.py:40
  138.2 252.1 %all-gather.12.cloned.1.call-start = ((), (), s32[]{:S(2)}) async-start(), calls=%async_computation.13 | async-start | bytes 2949120 | tf_op jit(solution)/shard_map/all_gather | solution.py:153
  253.2 9.2 %copy-start.1 = (bf16[1,1024,1280]{1,2,0:T(8,128)(2,1)S(1)}, bf16[1,1024,1280]{1,2,0:T(8,128)(2,1)}, u32[]{:S(2)}) copy-start(bf16[1,1024,1280]{1,2,0:T(8,128)(2,1)} %copy.24) | copy-start | bytes 7864324
  262.4 6.2 %copy-start = (bf16[2,16,40,1280]{3,2,0,1:T(8,128)(2,1)S(1)}, bf16[2,16,40,1280]{3,2,0,1:T(8,128)(2,1)}, u32[]{:S(2)}) copy-start(bf16[2,16,40,1280]{3,2,0,1:T(8,128)(2,1)} %copy.28) | copy-start | bytes 9830404
  268.6 1.0 copy-start.9
  268.7 2.0 copy-start.6
  270.6 174.9 %reduce-scatter.3.cloned.1.call-start = ((), (), s32[]{:S(2)}) async-start(), calls=%async_computation.11 | async-start | bytes 3276800 | tf_op jit(solution)/shard_map/reduce_scatter | solution.py:54
  412.2 33.3 %copy-start.11 = (f32[1000]{0:T(1024)S(1)}, f32[1000]{0:T(1024)}, u32[]{:S(2)}) copy-start(f32[1000]{0:T(1024)} %param.16) | copy-start | bytes 12004
  412.2 67.0 %reduce-scatter.5.cloned.1.call-start = ((), (), s32[]{:S(2)}) async-start(), calls=%async_computation.12 | async-start | bytes 983040 | tf_op jit(solution)/shard_map/reduce_scatter | solution.py:54
Sparse Core Ops, SparseCore 0:
  38.5 65.4 all-gather.5
  110.3 98.7 all-gather.7
  211.0 93.0 all-gather.9
  307.1 83.1 all-gather.11
  412.3 33.1 reduce-scatter.2
  447.8 31.2 reduce-scatter.4
